TPU v7x, 256 devices: a whole 4x4x8 slice. The times are simulated.
256 devices in a mesh: rows: 64 (over z, x, core), feat: 4 (over y).
Axes of the slice: x: 4, y: 4, z: 8, core: 2. Of those that a mesh axis runs over, the one named last changes fastest.
Arguments:
- predictions: bfloat16 [98304, 4096], P('rows', 'feat'), may hold values from -6 to 6
- labels: bfloat16 [98304, 4096], P('rows', 'feat'), may hold values from 0 to 1
- feature_codes: int32 [32, 98304], P('feat', 'rows'), may hold values from 0 to 255
- leaf_index: int32 [98304], P('rows'), may hold values from 0 to 63
- sketch_weight: bfloat16 [4096, 256], P('feat'), may hold values from -0.09375 to 0.09375
Outputs:
- histograms: float32 [256, 32, 256], P('rows', 'feat')
- leaf_values: float32 [64, 4096], P(None, 'feat')
- updated: bfloat16 [98304, 4096], P('rows', 'feat')
All inputs are finite; a program needn't handle non-finite values.
Results may differ from a plain program's by a relative error of at most 0.008.
Values may be sent and summed in bfloat16 or wider, within the bound.
A program may use at most 64 MiB of HBM per device.

v0:
```python
import jax
import jax.numpy as jnp
from jax import lax
from jax.sharding import PartitionSpec as P

BINS = 256
LEAVES = 64


shrinkage = 0.5
ridge_term = 1.0


def local(predictions, labels, feature_codes, leaf_index, sketch_weight):
    logits = predictions.astype(jnp.float32)
    probability = jax.nn.sigmoid(logits)
    gradient = (labels.astype(jnp.float32) - probability).astype(jnp.bfloat16)
    hessian = (probability * (1.0 - probability)).astype(jnp.bfloat16)
    partial_sketch = jnp.dot(gradient, sketch_weight, preferred_element_type=jnp.float32)
    partial_sketch = partial_sketch.astype(jnp.bfloat16)
    sketch = lax.psum(partial_sketch, "feat").astype(jnp.float32).astype(jnp.bfloat16)
    owned_bins = BINS // lax.axis_size("rows")
    levels = jnp.arange(BINS, dtype=jnp.int32)
    one_hot = (levels[:, None, None] == feature_codes[None, :, :]).astype(jnp.bfloat16)
    every_bin = lax.psum(
        jnp.einsum("bfr,rk->bfk", one_hot, sketch, preferred_element_type=jnp.float32), "rows"
    )
    histograms = lax.dynamic_slice_in_dim(
        every_bin, lax.axis_index("rows") * owned_bins, owned_bins, 0
    )
    leaf_hot = jnp.arange(LEAVES, dtype=jnp.int32)[:, None] == leaf_index[None, :]
    leaf_weights = leaf_hot.astype(jnp.bfloat16)
    grad_sum = jnp.dot(leaf_weights, gradient, preferred_element_type=jnp.float32)
    hess_sum = jnp.dot(leaf_weights, hessian, preferred_element_type=jnp.float32)
    grad_total, hess_total = lax.psum((grad_sum, hess_sum), "rows")
    leaf_values = grad_total / (hess_total + ridge_term)
    looked_up = jnp.einsum(
        "lr,lc->rc", leaf_hot.astype(jnp.float32), leaf_values, precision=lax.Precision.HIGHEST
    )
    updated = (logits + shrinkage * looked_up).astype(jnp.bfloat16)
    return (histograms, leaf_values, updated)


def solution(mesh):
    return jax.shard_map(
        local,
        mesh=mesh,
        in_specs=(
            P("rows", "feat"),
            P("rows", "feat"),
            P("feat", "rows"),
            P("rows"),
            P("feat", None),
        ),
        out_specs=(P("rows", "feat", None), P(None, "feat"), P("rows", "feat")),
        check_vma=False,
    )
```

profile of v0, /device:TPU:6, one launch (start us, length us, event | category | flops | bytes accessed | tf_op | source)
XLA Modules:
  0.0 280.2 jit_solution(7127721049263622959)
XLA Ops:
  7.2 0.0 copy-start
  7.2 0.0 all-reduce.4.cloned.1.call-start
  7.2 4.9 %subtract_convert_fusion = bf16[1536,1024]{1,0:T(8,128)(2,1)S(1)} fusion(bf16[1536,1024]{1,0:T(8,128)(2,1)} %param.6, bf16[1536,1024]{1,0:T(8,128)(2,1)} %param.5), kind=kLoop, calls=%fused_computation.10 | loop fusion | flops 11010048 | bytes 9437184 | tf_op jit(solution)/shard_map/convert_element_type | solution.py:17
  12.2 0.0 copy-start.2
  12.2 1.7 copy-done.2
  13.8 0.0 copy-done
  13.9 0.0 copy-start.4
  13.9 1.9 convolution_convert_fusion
  15.7 0.0 all-reduce.4.cloned.1.call-update
  15.8 0.0 all-reduce.6.cloned.1.call-start
  15.8 0.0 copy-done.4
  15.8 0.0 copy-start.1
  15.8 3.4 %fusion.12 = f32[64,1024]{1,0:T(8,128)} fusion(bf16[1536,1024]{1,0:T(8,128)(2,1)} %copy-done.2, s32[1536]{0:T(1024)S(1)} %copy-done.4), kind=kOutput, calls=%fused_computation.17 | convolution fusion | flops 201424896 | bytes 3414016 | tf_op jit(solution)/shard_map/dot_general | solution.py:33
  19.2 0.0 copy-done.1
  19.2 0.0 copy-start.5
  19.2 2.6 fusion.7
  21.8 46.6 %all-reduce.4.cloned.1.call-done = bf16[1536,256]{1,0:T(8,128)(2,1)} async-done(((bf16[1536,256]{1,0:T(8,128)(2,1)}), bf16[1536,256]{1,0:T(8,128)(2,1)}) %all-reduce.4.cloned.1.call-update) | async-done | bytes 786448 | tf_op jit(solution)/shard_map/psum | solution.py:21
  68.4 0.0 copy-done.5
  68.4 4.8 %fusion = f32[256,8,256]{2,0,1:T(8,128)} fusion(s32[8,1536]{1,0:T(8,128)S(1)} %copy-done.5, bf16[1536,256]{1,0:T(8,128)(2,1)} %all-reduce.4.cloned.1.call-done), kind=kOutput, calls=%fused_computation.1 | convolution fusion | flops 1613758464 | bytes 2932736 | tf_op jit(solution)/shard_map/bfr,rk->bfk/dot_general | solution.py:26
  73.2 0.0 all-reduce.6.cloned.1.call-update
  73.3 191.8 %all-reduce.6.cloned.1.call-done = (f32[256,8,256]{2,0,1:T(8,128)}, f32[64,1024]{1,0:T(8,128)}, f32[64,1024]{1,0:T(8,128)}) async-done(((f32[256,8,256]{2,0,1:T(8,128)}, f32[64,1024]{1,0:T(8,128)}, f32[64,1024]{1,0:T(8,128)}), (f32[256,8,256]{2,0,1:T(8,128)}, f32[64,1024]{1,0:T(8,128)}, f32[64,1024]{1,0:T(8,128)})) %all-reduce.6.cloned.1.call-update) | async-done | bytes 2621456 | tf_op jit(solution)/shard_map/psum | solution.py:25
  265.1 0.8 constant_dynamic-slice_fusion
  265.9 0.6 copy.8
  266.5 1.1 add_divide_fusion
  267.6 0.0 copy-start.3
  267.6 5.7 %fusion.4 = bf16[1536,1024]{1,0:T(8,128)(2,1)} fusion(bf16[1536,1024]{1,0:T(8,128)(2,1)} %param.5, f32[64,1024]{1,0:T(8,128)S(1)} %add_divide_fusion, s32[1536]{0:T(1024)S(1)} %copy-done.4), kind=kOutput, calls=%fused_computation.8 | convolution fusion | flops 1214349312 | bytes 6559744 | tf_op jit(solution)/shard_map/lr,lc->rc/dot_general | solution.py:37
  273.4 0.0 copy-done.3
Async XLA Ops:
  7.2 6.7 %copy-start = (bf16[1024,256]{1,0:T(8,128)(2,1)S(1)}, bf16[1024,256]{1,0:T(8,128)(2,1)}, u32[]{:S(2)}) copy-start(bf16[1024,256]{1,0:T(8,128)(2,1)} %param.9) | copy-start | bytes 1572868
  7.2 61.2 %all-reduce.4.cloned.1.call-start = ((), (), s32[]{:S(2)}) async-start(), calls=%async_computation | async-start | bytes 1572864 | tf_op jit(solution)/shard_map/psum | solution.py:21
  12.2 1.7 copy-start.2
  13.9 2.0 copy-start.4
  15.8 249.3 %all-reduce.6.cloned.1.call-start = ((), (), s32[]{:S(2)}) async-start(), calls=%async_computation.1 | async-start | bytes 5242880 | tf_op jit(solution)/shard_map/psum | solution.py:25
  15.8 3.4 %copy-start.1 = (bf16[1536,1024]{1,0:T(8,128)(2,1)S(1)}, bf16[1536,1024]{1,0:T(8,128)(2,1)}, u32[]{:S(2)}) copy-start(bf16[1536,1024]{1,0:T(8,128)(2,1)} %param.5) | copy-start | bytes 9437188
  19.2 49.1 %copy-start.5 = (s32[8,1536]{1,0:T(8,128)S(1)}, s32[8,1536]{1,0:T(8,128)}, u32[]{:S(2)}) copy-start(s32[8,1536]{1,0:T(8,128)} %param.7) | copy-start | bytes 147460
  267.6 5.8 %copy-start.3 = (f32[64,1024]{1,0:T(8,128)}, f32[64,1024]{1,0:T(8,128)S(1)}, u32[]{:S(2)}) copy-start(f32[64,1024]{1,0:T(8,128)S(1)} %add_divide_fusion) | copy-start | bytes 786436
Sparse Core Ops, SparseCore 0:
  15.9 52.4 all-reduce.3
  73.4 191.6 all-reduce.5
where the time goes:
time: 282 us; the launch traced here: 280 us
  waiting for transfers between devices  238 us (84%)
  matrix products  18.4 us (7%)
  between operations  14.1 us (5%)
  other arithmetic  6.02 us (2%)
  local copies, waits for them, and re-layouts  3.16 us (1%)
    psum x1, waiting for transfers between devices, local(): lax.psum(jnp.einsum('bfr,rk->bfk', one_hot, sketch, preferred_element_typ...  192 us
    psum x1, waiting for transfers between devices, local(): lax.psum(partial_sketch, 'feat').astype(jnp.float32).astype(jnp.bfloat16)  46.6 us
    dot_general x1, matrix products, local(): jnp.einsum('lr,lc->rc', leaf_hot.astype(jnp.float32), leaf_values, precis...  5.75 us
  transfers between devices with their start and end apart: 2, of which 2 were waited for; matrix products, arithmetic and copies ran while one was open for 2% of the time, Pallas kernels for 0%

commit v1 on v0

v1 whole, which is shorter than its diff:
```python
import jax
import jax.numpy as jnp
from jax import lax
from jax.experimental import pallas as pl
from jax.experimental.pallas import tpu as pltpu
from jax.sharding import PartitionSpec as P

BINS = 256
LEAVES = 64
NZ, NX, NC, NY = 8, 4, 2, 4
R, L, K, F = 1536, 1024, 256, 8
Q = R // NY
H = Q // 2
OWN = BINS // LEAVES * F
PIECE = NZ * OWN
MESH = pl.DeviceIdType.MESH
F32, BF16 = jnp.float32, jnp.bfloat16

shrinkage = 0.5
ridge_term = 1.0

RS, AG, LC, LX, LZ, VX, VC, HC, HX, HZ = 0, 6, 12, 13, 16, 23, 26, 27, 31, 37
COPIES = 44


def owner(slot):
    return (slot & 7) * 8 + ((slot >> 3) & 3) * 2 + (slot >> 5)


def kernel(pred_hbm, lab_hbm, codes_hbm, leaf_hbm, w_hbm,
           hist_ref, value_ref, upd_ref,
           pred, lab, codes, leaf, w, grad, hess, part, rs1, rs2, rsum, sk, hot, oh,
           lsum, lcs, lcr, lxs, lxr, lz, lv, acc, hcs, hcr, hxs, hx1, hx2, hxsum, hzs, hzr,
           load_sem, send, recv):
    row = lax.axis_index("rows")
    y = lax.axis_index("feat")
    c = lax.rem(row, NC)
    x = lax.rem(row // NC, NX)
    z = row // (NC * NX)

    def at(zz, xx, cc):
        return (zz * NX + xx) * NC + cc

    def step(v, d, n):
        return lax.rem(v + d, n)

    partner = (at(z, x, 1 - c), y)
    ypeer = [(row, step(y, d, NY)) for d in range(NY)]
    xpeer = [(at(z, step(x, d, NX), c), y) for d in range(NX)]
    zpeer = [(at(step(z, d, NZ), x, c), y) for d in range(NZ)]

    def copy(n, src, dst, to):
        return pltpu.make_async_remote_copy(
            src_ref=src, dst_ref=dst, send_sem=send.at[n], recv_sem=recv.at[n],
            device_id=to, device_id_type=MESH)

    barrier = pltpu.get_barrier_semaphore()
    peers = [partner] + ypeer[1::2] + xpeer[1:] + zpeer[1:]
    for peer in peers:
        pl.semaphore_signal(barrier, inc=1, device_id=peer, device_id_type=MESH)

    order = [step(y, 2, NY), step(y, 1, NY), step(y, 3, NY), y]
    loads = []
    for i, q in enumerate(order):
        rows = pl.ds(pl.multiple_of(q * Q, Q), Q)
        loads.append((
            pltpu.make_async_copy(pred_hbm.at[rows], pred.at[q], load_sem.at[2 * i]),
            pltpu.make_async_copy(lab_hbm.at[rows], lab.at[q], load_sem.at[2 * i + 1]),
        ))
    small = [
        pltpu.make_async_copy(leaf_hbm, leaf, load_sem.at[8]),
        pltpu.make_async_copy(w_hbm, w, load_sem.at[9]),
        pltpu.make_async_copy(codes_hbm, codes, load_sem.at[10]),
    ]
    small[0].start()
    for cp in loads[0]:
        cp.start()
    small[1].start()
    for cp in loads[1] + loads[2] + loads[3]:
        cp.start()
    small[2].start()
    small[0].wait()

    slots = lax.broadcasted_iota(jnp.int32, (LEAVES, Q), 0)
    lane_owner = owner(slots)
    for q in range(NY):
        here = leaf[:, q * Q:(q + 1) * Q] == lane_owner
        hot[q] = jnp.where(here, 1.0, 0.0).astype(BF16)

    def block(i):
        q = order[i]
        for cp in loads[i]:
            cp.wait()

        def rows16(j, carry):
            rows = pl.ds(pl.multiple_of(j * 16, 16), 16)
            logits = pred[q, rows, :].astype(F32)
            probability = 0.5 + 0.5 * jnp.tanh(0.5 * logits)
            grad[rows, :] = (lab[q, rows, :].astype(F32) - probability).astype(BF16)
            hess[rows, :] = (probability * (1.0 - probability)).astype(BF16)
            return carry

        lax.fori_loop(0, Q // 16, rows16, 0)
        if i == 0:
            small[1].wait()
        part[q] = jnp.dot(grad[...], w[...], preferred_element_type=F32).astype(BF16)

    def leaf_sums(i):
        q = order[i]
        for n, src in ((0, grad), (1, hess)):
            cols = pl.ds(n * L, L)
            s = jnp.dot(hot[q], src[...], preferred_element_type=F32)
            lsum[:, cols] = s if i == 0 else lsum[:, cols] + s

    top, low = pl.ds(0, H), pl.ds(H, H)
    q2, q1, q3, q0 = order
    rs = [
        copy(RS + 0, part.at[q2, top], rs1.at[0], ypeer[1]),
        copy(RS + 1, part.at[q2, low], rs1.at[1], ypeer[3]),
        copy(RS + 2, part.at[q1, low], rs2.at[0, 1], ypeer[1]),
        copy(RS + 3, part.at[q3, top], rs2.at[1, 0], ypeer[3]),
        copy(RS + 4, rsum.at[0], rs2.at[0, 0], ypeer[1]),
        copy(RS + 5, rsum.at[1], rs2.at[1, 1], ypeer[3]),
    ]
    block(0)
    pl.semaphore_wait(barrier, len(peers))
    rs[0].start()
    rs[1].start()
    leaf_sums(0)
    block(1)
    rs[2].start()
    leaf_sums(1)
    block(2)
    rs[3].start()
    leaf_sums(2)
    rs[0].wait_recv()
    rsum[0] = (part[q1, top, :].astype(F32) + rs1[0].astype(F32)).astype(BF16)
    rs[4].start()
    rs[1].wait_recv()
    rsum[1] = (part[q3, low, :].astype(F32) + rs1[1].astype(F32)).astype(BF16)
    rs[5].start()
    block(3)
    leaf_sums(3)

    give, keep = pl.ds((1 - c) * 32, 32), pl.ds(c * 32, 32)
    given = lsum[pl.ds(pl.multiple_of((1 - c) * 32, 32), 32), :].astype(BF16)
    for i in range(NX):
        lcs[i] = given[i * 8:(i + 1) * 8, :]
    lc = copy(LC, lcs, lcr, partner)
    lc.start()

    small[2].wait()
    offset = jnp.where(lax.broadcasted_iota(jnp.int32, (16, R), 0) >= 8, 1, 0)
    pair = (jnp.concatenate([codes[...], codes[...]], axis=0) - offset).astype(BF16)

    def bins_of(s, carry):
        first = owner(s) * 4
        for b in (0, 2):
            level = jnp.full((16, R), first + b, jnp.int32).astype(BF16)
            ones = jnp.where(pair == level, jnp.ones((), BF16), jnp.zeros((), BF16))
            rows = pl.ds(pl.multiple_of(s * 32 + b * 8, 16), 16)
            for q in range(NY):
                oh[q, rows, :] = ones[:, q * Q:(q + 1) * Q]
        return carry

    lax.fori_loop(0, LEAVES, bins_of, 0)

    rs[3].wait_recv()
    rs[4].wait_recv()
    own = part[q0, top, :].astype(F32) + rs2[0, 0].astype(F32) + rs2[1, 0].astype(F32)
    sk[q0, top, :] = own.astype(BF16)
    ag = [
        copy(AG + 0, sk.at[q0, top], sk.at[q0, top], ypeer[1]),
        copy(AG + 1, sk.at[q0, low], sk.at[q0, low], ypeer[3]),
        copy(AG + 2, sk.at[q0, low], sk.at[q0, low], ypeer[1]),
        copy(AG + 3, sk.at[q0, top], sk.at[q0, top], ypeer[3]),
        copy(AG + 4, sk.at[q3, top], sk.at[q3, top], ypeer[1]),
        copy(AG + 5, sk.at[q1, low], sk.at[q1, low], ypeer[3]),
    ]

    def arrival(n, dst):
        copy(n, dst, dst, partner).wait_recv()

    ag[0].start()
    rs[2].wait_recv()
    rs[5].wait_recv()
    own = part[q0, low, :].astype(F32) + rs2[0, 1].astype(F32) + rs2[1, 1].astype(F32)
    sk[q0, low, :] = own.astype(BF16)
    ag[1].start()
    ag[2].start()
    ag[3].start()

    lc.wait_recv()
    kept = lsum[pl.ds(pl.multiple_of(c * 32, 32), 32), :]
    for i in range(NX):
        lsum[pl.ds(i * 8, 8), :] = kept[i * 8:(i + 1) * 8, :] + lcr[i].astype(F32)
    lx = []
    for d in (2, 1, 3):
        to = step(x, d, NX)
        lxs[d - 1] = lsum[pl.ds(pl.multiple_of(to * 8, 8), 8), :].astype(BF16)
        lx.append(copy(LX + d - 1, lxs.at[d - 1], lxr.at[d - 1], xpeer[d]))
        lx[-1].start()

    def add_hist(q, m, first):
        rows = pl.ds(pl.multiple_of(m * PIECE, PIECE), PIECE)
        s = jnp.dot(oh[q, rows, :], sk[q], preferred_element_type=F32)
        return s if first else acc[rows, :] + s

    def hist_of(q, first=False):
        def body(m, carry):
            rows = pl.ds(pl.multiple_of(m * PIECE, PIECE), PIECE)
            acc[rows, :] = add_hist(q, m, first)
            return carry

        lax.fori_loop(0, NC * NX, body, 0)

    hist_of(q0, True)

    for cp in lx:
        cp.wait_recv()
    mine = lsum[pl.ds(pl.multiple_of(x * 8, 8), 8), :]
    for d in range(3):
        mine = mine + lxr[d].astype(F32)
    lz[z] = mine.astype(BF16)
    lzc = [copy(LZ + d - 1, lz.at[z], lz.at[z], zpeer[d]) for d in (4, 3, 5, 2, 6, 1, 7)]
    for cp in lzc:
        cp.start()

    arrival(AG + 0, sk.at[q3, top])
    ag[4].start()
    arrival(AG + 1, sk.at[q1, low])
    ag[5].start()
    arrival(AG + 2, sk.at[q3, low])
    hist_of(q3)
    arrival(AG + 3, sk.at[q1, top])
    hist_of(q1)
    arrival(AG + 4, sk.at[q2, top])
    arrival(AG + 5, sk.at[q2, low])

    xorder = [step(x, 2, NX), step(x, 1, NX), step(x, 3, NX), x]
    hc = []
    for i, to in enumerate(xorder):
        hcs[to] = add_hist(q2, (1 - c) * NX + to, False).astype(BF16)
        hc.append(copy(HC + i, hcs.at[to], hcr.at[to], partner))
        hc[-1].start()
    for to in xorder:
        acc[pl.ds(pl.multiple_of(to * PIECE, PIECE), PIECE), :] = add_hist(q2, c * NX + to, False)

    def piece(i):
        hc[i].wait_recv()
        to = xorder[i]
        return acc[pl.ds(pl.multiple_of(to * PIECE, PIECE), PIECE), :] + hcr[to].astype(F32)

    half = PIECE // 2
    up, down = pl.ds(0, half), pl.ds(half, half)
    hx = [
        copy(HX + 0, hxs.at[0, up], hx1.at[0], xpeer[1]),
        copy(HX + 1, hxs.at[0, down], hx1.at[1], xpeer[3]),
        copy(HX + 2, hxs.at[1, down], hx2.at[0, 1], xpeer[1]),
        copy(HX + 3, hxs.at[2, up], hx2.at[1, 0], xpeer[3]),
        copy(HX + 4, hxsum.at[0], hx2.at[0, 0], xpeer[1]),
        copy(HX + 5, hxsum.at[1], hx2.at[1, 1], xpeer[3]),
    ]
    hxs[0] = piece(0).astype(BF16)
    hx[0].start()
    hx[1].start()
    right = piece(1)
    hxs[1, down, :] = right[half:, :].astype(BF16)
    hx[2].start()
    left = piece(2)
    hxs[2, up, :] = left[:half, :].astype(BF16)
    hx[3].start()
    spare = NX * PIECE
    acc[pl.ds(spare, half), :] = right[:half, :]
    acc[pl.ds(spare + half, half), :] = left[half:, :]
    acc[pl.ds(spare + PIECE, PIECE), :] = piece(3)
    hx[0].wait_recv()
    hxsum[0] = (acc[pl.ds(spare, half), :] + hx1[0].astype(F32)).astype(BF16)
    hx[4].start()
    hx[1].wait_recv()
    hxsum[1] = (acc[pl.ds(spare + half, half), :] + hx1[1].astype(F32)).astype(BF16)
    hx[5].start()

    for cp, d in zip(lzc, (4, 3, 5, 2, 6, 1, 7)):
        arrival(LZ + d - 1, lz.at[step(z, NZ - d, NZ)])
    total = lz[0].astype(F32)
    for i in range(1, NZ):
        total = total + lz[i].astype(F32)
    values = (total[:, :L] / (total[:, L:] + ridge_term)).astype(BF16)
    lv[c, x] = values
    vx = [copy(VX + d - 1, lv.at[c, x], lv.at[c, x], xpeer[d]) for d in (2, 1, 3)]
    for cp in vx:
        cp.start()

    for n in (3, 4, 2, 5):
        hx[n].wait_recv()
    for i, rows in enumerate((up, down)):
        s = acc[pl.ds(spare + PIECE + i * half, half), :] + hx2[0, i].astype(F32) + hx2[1, i].astype(F32)
        acc[pl.ds(i * half, half), :] = s
    hz = []
    for d in (4, 3, 5, 2, 6, 1, 7):
        to = step(z, d, NZ)
        hzs[d - 1] = acc[pl.ds(pl.multiple_of(to * OWN, OWN), OWN), :].astype(BF16)
        hz.append(copy(HZ + d - 1, hzs.at[d - 1], hzr.at[d - 1], zpeer[d]))
        hz[-1].start()

    for d in (2, 1, 3):
        arrival(VX + d - 1, lv.at[c, step(x, NX - d, NX)])
    vc = copy(VC, lv.at[c], lv.at[c], partner)
    vc.start()
    arrival(VC, lv.at[1 - c])

    table = jnp.concatenate([lv[i, j] for i in range(NC) for j in range(NX)], axis=0)
    spot = lax.broadcasted_iota(jnp.int32, (LEAVES, LEAVES), 1)
    label = lax.broadcasted_iota(jnp.int32, (LEAVES, LEAVES), 0)
    swap = jnp.where(owner(spot) == label, 1.0, 0.0).astype(BF16)
    value_ref[...] = jnp.dot(swap, table, preferred_element_type=F32)

    for q in range(NY):
        looked_up = lax.dot_general(hot[q], table, (((0,), (0,)), ((), ())),
                                    preferred_element_type=F32)
        upd_ref[pl.ds(q * Q, Q), :] = (pred[q].astype(F32) + shrinkage * looked_up).astype(BF16)

    s = acc[pl.ds(pl.multiple_of(z * OWN, OWN), OWN), :]
    for i, d in enumerate((4, 3, 5, 2, 6, 1, 7)):
        hz[i].wait_recv()
        s = s + hzr[d - 1].astype(F32)
    hist_ref[...] = s

    for cp in rs + ag + [lc] + lx + lzc + hc + hx + vx + hz + [vc]:
        cp.wait_send()


def local(predictions, labels, feature_codes, leaf_index, sketch_weight):
    vmem = lambda *shape, kind=BF16: pltpu.VMEM(shape, kind)
    hist, values, updated = pl.pallas_call(
        kernel,
        out_shape=(
            jax.ShapeDtypeStruct((OWN, K), F32),
            jax.ShapeDtypeStruct((LEAVES, L), F32),
            jax.ShapeDtypeStruct((R, L), BF16),
        ),
        in_specs=[pl.BlockSpec(memory_space=pl.ANY)] * 5,
        out_specs=[pl.BlockSpec(memory_space=pltpu.VMEM)] * 3,
        scratch_shapes=[
            vmem(NY, Q, L), vmem(NY, Q, L), vmem(F, R, kind=jnp.int32), vmem(1, R, kind=jnp.int32), vmem(L, K),
            vmem(Q, L), vmem(Q, L), vmem(NY, Q, K), vmem(2, H, K), vmem(2, 2, H, K), vmem(2, H, K),
            vmem(NY, Q, K), vmem(NY, LEAVES, Q), vmem(NY, BINS * F, Q),
            vmem(LEAVES, 2 * L, kind=F32), vmem(NX, 8, 2 * L), vmem(NX, 8, 2 * L), vmem(3, 8, 2 * L),
            vmem(3, 8, 2 * L), vmem(NZ, 8, 2 * L), vmem(NC, NX, 8, L),
            vmem(BINS * F, K, kind=F32), vmem(NX, PIECE, K), vmem(NX, PIECE, K), vmem(3, PIECE, K),
            vmem(2, PIECE // 2, K), vmem(2, 2, PIECE // 2, K), vmem(2, PIECE // 2, K),
            vmem(7, OWN, K), vmem(7, OWN, K),
            pltpu.SemaphoreType.DMA((11,)), pltpu.SemaphoreType.DMA((COPIES,)), pltpu.SemaphoreType.DMA((COPIES,)),
        ],
        compiler_params=pltpu.CompilerParams(
            collective_id=0, has_side_effects=True, vmem_limit_bytes=56 * 2**20),
        name="boost",
    )(predictions, labels, feature_codes, leaf_index.reshape(1, R), sketch_weight)
    return hist.reshape(BINS // LEAVES, F, K), values, updated


def solution(mesh):
    return jax.shard_map(
        local,
        mesh=mesh,
        in_specs=(
            P("rows", "feat"),
            P("rows", "feat"),
            P("feat", "rows"),
            P("rows"),
            P("feat", None),
        ),
        out_specs=(P("rows", "feat", None), P(None, "feat"), P("rows", "feat")),
        check_vma=False,
    )
```

time: 282 us -> 53.9 us (0.19)
  waiting for transfers between devices: 238 us -> 0 us
  Pallas kernels: 0 us -> 44.8 us
  matrix products: 18.4 us -> 0 us
  between operations: 14.1 us -> 0.64 us
  other arithmetic: 6.02 us -> 0 us
  local copies, waits for them, and re-layouts: 3.16 us -> 8.2 us
    psum x2 -> x0, waiting for transfers between devices: 238 us -> none  [the longest x1 192 us: local(): lax.psum(jnp.einsum('bfr,rk->bfk', one_hot, sketch, preferred_element_typ...]
    pallas_call x0 -> x1, Pallas kernels: none -> 44.8 us  [local(): pl.pallas_call(kernel, out_shape=(jax.ShapeDtypeStruct((OWN, K), F32), ja...]
    dot_general x5 -> x0, matrix products: 18.4 us -> none  [the longest x1 5.75 us: local(): jnp.einsum('lr,lc->rc', leaf_hot.astype(jnp.float32), leaf_values, precis...]
    convert_element_type x1 -> x0, other arithmetic: 4.95 us -> none  [local(): gradient = (labels.astype(jnp.float32) - probability).astype(jnp.bfloat16)]
    unnamed x13 -> x3, local copies, waits for them, and re-layouts: 2.31 us -> 6.9 us
  transfers between devices with their start and end apart: 2 -> 0, of which waited for: 2 -> 0; matrix products, arithmetic and copies ran while one was open for 2% -> 0% of each run, Pallas kernels for 0% -> 0%
where the time goes in v1:
time: 53.9 us; the launch traced here: 53.6 us
  Pallas kernels  44.8 us (83%)
  local copies, waits for them, and re-layouts  8.2 us (15%)
  between operations  0.64 us (1%)
    pallas_call x1, Pallas kernels, local(): pl.pallas_call(kernel, out_shape=(jax.ShapeDtypeStruct((OWN, K), F32), ja...  44.8 us
    unnamed x3, local copies, waits for them, and re-layouts  6.9 us
    reshape x1, local copies, waits for them, and re-layouts, local(): leaf_index.reshape(1, R)  1.3 us

profile of v1, /device:TPU:6, one launch (start us, length us, event | category | flops | bytes accessed | tf_op | source)
XLA Modules:
  0.0 53.6 jit_solution(12290836009886620318)
XLA Ops:
  0.6 1.3 %reshape.12.leaf_hbm = s32[1,1536]{1,0:T(1,128)} reshape(s32[1536]{0:T(1024)} %param.8) | data formatting | bytes 12288 | tf_op jit(solution)/shard_map/reshape | solution.py:359
  1.9 44.8 %boost.1 = (f32[32,256]{1,0:T(8,128)}, f32[64,1024]{1,0:T(8,128)}, bf16[1536,1024]{1,0:T(8,128)(2,1)}) custom-call(bf16[1536,1024]{1,0:T(8,128)(2,1)} %pred_hbm.1, bf16[1536,1024]{1,0:T(8,128)(2,1)} %lab_hbm.1, s32[8,1536]{1,0:T(8,128)} %codes_hbm.1, s32[1,1536]{1,0:T(1,128)} %reshape.12.leaf_hbm, bf16[1024,256]{1,0:T(8,128)(2,1)} %w_hbm.1), custom_call_target="tpu_custom_call" | custom-call | tf_op jit(solution)/shard_map/boost/pallas_call | solution.py:336
  46.7 1.4 %copy.11 = f32[4,8,256]{2,1,0:T(8,128)} copy(f32[4,8,256]{2,1,0:T(8,128)} %bitcast.1) | data formatting | bytes 65536
  48.1 1.7 %copy.12 = f32[64,1024]{1,0:T(8,128)} copy(f32[64,1024]{1,0:T(8,128)} %get-tuple-element.13) | data formatting | bytes 524288
  49.7 3.9 %copy.13 = bf16[1536,1024]{1,0:T(8,128)(2,1)} copy(bf16[1536,1024]{1,0:T(8,128)(2,1)} %get-tuple-element.14) | data formatting | bytes 6291456

commit v2 on v0

v2 whole, which is shorter than its diff:
```python
import jax
import jax.numpy as jnp
from jax import lax
from jax.experimental import pallas as pl
from jax.experimental.pallas import tpu as pltpu
from jax.sharding import PartitionSpec as P

BINS = 256
LEAVES = 64
NZ, NX, NC, NY = 8, 4, 2, 4
R, L, K, F = 1536, 1024, 256, 8
HALVES = 2
W = K // HALVES
Q = R // NY
H = Q // 2
OWN = BINS // LEAVES * F
PIECE = NZ * OWN
CORE = NX * PIECE
MESH = pl.DeviceIdType.MESH
F32, BF16 = jnp.float32, jnp.bfloat16

shrinkage = 0.5
ridge_term = 1.0

RS, AG, HC, HX, HZ, PER_HALF = 0, 6, 12, 16, 22, 29
LC, LX, LZ, VZ, VX, COPIES = 58, 59, 62, 69, 76, 83
FAR_FIRST = (4, 3, 5, 2, 6, 1, 7)
XORDER = (2, 1, 3, 0)


def leaf_of(slot):
    return (slot & 7) * 8 + ((slot >> 3) & 3) * 2 + (slot >> 5)


def kernel(pred_hbm, lab_hbm, codes_hbm, leaf_hbm, w_hbm,
           hist_ref, value_ref, upd_ref,
           pred, lab, codes, leaf, w, grad, hess, part, rs1, rs2, rsum, sk, hot, oh,
           lsum, lcs, lcr, lxs, lxr, lzs, lzr, lvz, lv,
           acc, hcs, hcr, hxs, hx1, hx2, hxsum, fsum, hzs, hzr,
           load_sem, send, recv):
    row = lax.axis_index("rows")
    y = lax.axis_index("feat")
    c = lax.rem(row, NC)
    x = lax.rem(row // NC, NX)
    z = row // (NC * NX)

    def at(zz, xx, cc):
        return (zz * NX + xx) * NC + cc

    def step(v, d, n):
        return lax.rem(v + d, n)

    partner = (at(z, x, 1 - c), y)
    ypeer = [(row, step(y, d, NY)) for d in range(NY)]
    xpeer = [(at(z, step(x, d, NX), c), y) for d in range(NX)]
    zpeer = [(at(step(z, d, NZ), x, c), y) for d in range(NZ)]
    other = [(at(z, step(x, d, NX), 1 - c), y) for d in range(NX)]
    started = []

    def copy(n, src, dst, to):
        return pltpu.make_async_remote_copy(
            src_ref=src, dst_ref=dst, send_sem=send.at[n], recv_sem=recv.at[n],
            device_id=to, device_id_type=MESH)

    def go(n, src, dst, to):
        cp = copy(n, src, dst, to)
        cp.start()
        started.append(cp)

    def arrival(n, dst):
        copy(n, dst, dst, partner).wait_recv()

    def part_of(start, size, unit):
        return pl.ds(pl.multiple_of(start, unit), size)

    barrier = pltpu.get_barrier_semaphore()
    peers = other + ypeer[1::2] + xpeer[1:] + zpeer[1:]
    for peer in peers:
        pl.semaphore_signal(barrier, inc=1, device_id=peer, device_id_type=MESH)

    order = [step(y, 2, NY), step(y, 1, NY), step(y, 3, NY), y]
    w_load = pltpu.make_async_copy(w_hbm, w, load_sem.at[16])
    leaf_load = pltpu.make_async_copy(leaf_hbm, leaf, load_sem.at[17])
    codes_load = pltpu.make_async_copy(codes_hbm, codes, load_sem.at[18])
    loads = []
    for n in range(2 * NY):
        rows = part_of(order[n // 2] * Q + n % 2 * H, H, H)
        loads.append((
            pltpu.make_async_copy(pred_hbm.at[rows], pred.at[rows], load_sem.at[2 * n]),
            pltpu.make_async_copy(lab_hbm.at[rows], lab.at[rows], load_sem.at[2 * n + 1]),
        ))
        for cp in loads[-1]:
            cp.start()
        if n == 1:
            w_load.start()
    leaf_load.start()
    codes_load.start()

    def block(i):
        q = order[i]
        def rows16(j, carry):
            rows = part_of(q * Q + j * 16, 16, 16)
            logits = pred[rows, :].astype(F32)
            probability = 0.5 + 0.5 * jnp.tanh(0.5 * logits)
            grad[rows, :] = (lab[rows, :].astype(F32) - probability).astype(BF16)
            hess[rows, :] = (probability * (1.0 - probability)).astype(BF16)
            return carry

        for n in range(2):
            for cp in loads[2 * i + n]:
                cp.wait()
            lax.fori_loop(n * H // 16, (n + 1) * H // 16, rows16, 0, unroll=2)
        if i == 0:
            w_load.wait()
        sketch = jnp.dot(grad[part_of(q * Q, Q, Q), :], w[...], preferred_element_type=F32)
        for h in range(HALVES):
            part[h, i] = sketch[:, h * W:(h + 1) * W].astype(BF16)

    top, low = pl.ds(0, H), pl.ds(H, H)

    def rs_first(h):
        go(h * PER_HALF + RS + 0, part.at[h, 0, top], rs1.at[h, 0], ypeer[1])
        go(h * PER_HALF + RS + 1, part.at[h, 0, low], rs1.at[h, 1], ypeer[3])

    def rs_right(h):
        go(h * PER_HALF + RS + 2, part.at[h, 1, low], rs2.at[h, 0, 1], ypeer[1])

    def rs_left(h):
        go(h * PER_HALF + RS + 3, part.at[h, 2, top], rs2.at[h, 1, 0], ypeer[3])

    def rs_sums(h):
        arrival(h * PER_HALF + RS + 0, rs1.at[h, 0])
        rsum[h, 0] = (part[h, 1, top, :].astype(F32) + rs1[h, 0].astype(F32)).astype(BF16)
        go(h * PER_HALF + RS + 4, rsum.at[h, 0], rs2.at[h, 0, 0], ypeer[1])
        arrival(h * PER_HALF + RS + 1, rs1.at[h, 1])
        rsum[h, 1] = (part[h, 2, low, :].astype(F32) + rs1[h, 1].astype(F32)).astype(BF16)
        go(h * PER_HALF + RS + 5, rsum.at[h, 1], rs2.at[h, 1, 1], ypeer[3])

    def sk_at(h, slot, rows):
        return sk.at[h, slot, rows]

    def own_sketch(h):
        for n, rows, s, to, slot in ((0, top, 4, 1, 1), (1, low, 5, 3, 2)):
            arrival(h * PER_HALF + RS + s, rs2.at[h, n, n])
            arrival(h * PER_HALF + RS + (3, 2)[n], rs2.at[h, 1 - n, n])
            total = part[h, 3, rows, :].astype(F32) + rs2[h, 0, n].astype(F32) + rs2[h, 1, n].astype(F32)
            sk[h, 0, rows, :] = total.astype(BF16)
            go(h * PER_HALF + AG + n, sk_at(h, 0, rows), sk_at(h, slot, rows), ypeer[to])

    def own_rest(h):
        go(h * PER_HALF + AG + 2, sk_at(h, 0, low), sk_at(h, 1, low), ypeer[1])
        go(h * PER_HALF + AG + 3, sk_at(h, 0, top), sk_at(h, 2, top), ypeer[3])

    def forward(h):
        arrival(h * PER_HALF + AG + 0, sk_at(h, 1, top))
        go(h * PER_HALF + AG + 4, sk_at(h, 1, top), sk_at(h, 3, top), ypeer[1])
        arrival(h * PER_HALF + AG + 1, sk_at(h, 2, low))
        go(h * PER_HALF + AG + 5, sk_at(h, 2, low), sk_at(h, 3, low), ypeer[3])

    block(0)
    pl.semaphore_wait(barrier, len(peers))
    rs_first(0)
    rs_first(1)
    block(1)
    rs_right(0)
    block(2)
    rs_left(0)
    rs_sums(0)
    rs_right(1)
    rs_left(1)
    block(3)
    rs_sums(1)

    leaf_load.wait()
    lane_owner = leaf_of(lax.broadcasted_iota(jnp.int32, (LEAVES, R), 0))
    here = leaf[...].reshape(1, R) == lane_owner
    hot[...] = jnp.where(here, 1.0, 0.0).astype(BF16)
    for n, src in ((0, grad), (1, hess)):
        lsum[:, n * L:(n + 1) * L] = jnp.dot(hot[...], src[...], preferred_element_type=F32)

    given = lsum[part_of((1 - c) * 32, 32, 32), :].astype(BF16)
    for i in range(NX):
        lcs[i] = given[i * 8:(i + 1) * 8, :]
    go(LC, lcs, lcr, partner)

    own_sketch(0)
    own_rest(0)

    codes_load.wait()
    lanes = [codes[:, part_of(order[i] * Q, Q, 128)] for i in (3, 2, 1, 0)]
    level = jnp.concatenate(lanes, axis=1)
    offset = jnp.where(lax.broadcasted_iota(jnp.int32, (16, R), 0) >= 8, 1, 0)
    pair = (jnp.concatenate([level, level], axis=0) - offset).astype(BF16)

    def bins_of(zz, carry):
        for side in range(NC):
            for i, d in enumerate(XORDER):
                device = at(zz, step(x, d, NX), (1 - c) if side == 0 else c)
                for b in (0, 2):
                    bins = jnp.full((16, 128), device * 4 + b, jnp.int32).astype(BF16)
                    bins = jnp.concatenate([bins] * (R // 128), axis=1)
                    rows = part_of(side * CORE + i * PIECE + zz * OWN + b * 8, 16, 16)
                    oh[rows, :] = jnp.where(pair == bins, jnp.ones((), BF16), jnp.zeros((), BF16))
        return carry

    lax.fori_loop(0, NZ, bins_of, 0)

    arrival(LC, lcr)
    kept = lsum[part_of(c * 32, 32, 32), :]
    for i in range(NX):
        lsum[pl.ds(i * 8, 8), :] = kept[i * 8:(i + 1) * 8, :] + lcr[i].astype(F32)
    for d in (2, 1, 3):
        lxs[d - 1] = lsum[part_of(step(x, d, NX) * 8, 8, 8), :].astype(BF16)
        go(LX + d - 1, lxs.at[d - 1], lxr.at[d - 1], xpeer[d])

    own_sketch(1)
    own_rest(1)

    def terms(h, first, last, rows):
        sketch = sk[h, first:last].reshape((last - first) * Q, W)
        return jnp.dot(oh[rows, first * Q:last * Q], sketch, preferred_element_type=F32)

    tiles = [pl.ds(i * PIECE, PIECE) for i in range(NC * NX)]

    def start_terms(h):
        for rows in tiles:
            acc[h, rows, :] = terms(h, 0, 1, rows)

    def side_terms(h):
        arrival(h * PER_HALF + AG + 2, sk_at(h, 1, low))
        arrival(h * PER_HALF + AG + 3, sk_at(h, 2, top))
        for rows in tiles:
            acc[h, rows, :] = acc[h, rows, :] + terms(h, 1, 3, rows)

    start_terms(0)
    start_terms(1)
    forward(0)
    for d in (1, 2, 3):
        arrival(LX + d - 1, lxr.at[d - 1])
    mine = lsum[part_of(x * 8, 8, 8), :]
    for d in range(3):
        mine = mine + lxr[d].astype(F32)
    for i in range(NZ):
        lzs[i] = mine[i:i + 1, :]
    for d in FAR_FIRST:
        go(LZ + d - 1, lzs.at[step(z, d, NZ)], lzr.at[d - 1], zpeer[d])
    side_terms(0)
    forward(1)
    side_terms(1)

    def last_rows(h):
        arrival(h * PER_HALF + AG + 4, sk_at(h, 3, top))
        arrival(h * PER_HALF + AG + 5, sk_at(h, 3, low))
        for i in range(0, NX, 2):
            for j in (i, i + 1):
                hcs[h, j] = (acc[h, tiles[j], :] + terms(h, 3, 4, tiles[j])).astype(BF16)
            for j in (i, i + 1):
                go(h * PER_HALF + HC + j, hcs.at[h, j], hcr.at[h, j], partner)
        for rows in tiles[NX:]:
            acc[h, rows, :] = acc[h, rows, :] + terms(h, 3, 4, rows)

    half = PIECE // 2
    up, down = pl.ds(0, half), pl.ds(half, half)

    def both_cores(h, i, n):
        return acc[h, pl.ds(CORE + i * PIECE + n * half, half), :] + hcr[h, i, pl.ds(n * half, half), :].astype(F32)

    def x_first(h):
        for i in range(NX):
            arrival(h * PER_HALF + HC + i, hcr.at[h, i])
            if i == 0:
                hxs[h, 0] = both_cores(h, 0, 0).astype(BF16)
                hxs[h, 1] = both_cores(h, 0, 1).astype(BF16)
                go(h * PER_HALF + HX + 0, hxs.at[h, 0], hx1.at[h, 0], xpeer[1])
                go(h * PER_HALF + HX + 1, hxs.at[h, 1], hx1.at[h, 1], xpeer[3])
            if i == 1:
                hxs[h, 2] = both_cores(h, 1, 1).astype(BF16)
                go(h * PER_HALF + HX + 2, hxs.at[h, 2], hx2.at[h, 0, 1], xpeer[1])
            if i == 2:
                hxs[h, 3] = both_cores(h, 2, 0).astype(BF16)
                go(h * PER_HALF + HX + 3, hxs.at[h, 3], hx2.at[h, 1, 0], xpeer[3])

    def x_second(h):
        for n, i, to in ((0, 1, 1), (1, 2, 3)):
            arrival(h * PER_HALF + HX + n, hx1.at[h, n])
            hxsum[h, n] = (both_cores(h, i, n) + hx1[h, n].astype(F32)).astype(BF16)
            go(h * PER_HALF + HX + 4 + n, hxsum.at[h, n], hx2.at[h, n, n], xpeer[to])

    def z_only(h):
        for n in range(2):
            arrival(h * PER_HALF + HX + 4 + n, hx2.at[h, n, n])
            arrival(h * PER_HALF + HX + 3 - n, hx2.at[h, 1 - n, n])
        for n in range(2):
            fsum[h, pl.ds(n * half, half), :] = (
                both_cores(h, 3, n) + hx2[h, 0, n].astype(F32) + hx2[h, 1, n].astype(F32))
        for d in FAR_FIRST:
            hzs[h, d - 1] = fsum[h, part_of(step(z, d, NZ) * OWN, OWN, OWN), :].astype(BF16)
            go(h * PER_HALF + HZ + d - 1, hzs.at[h, d - 1], hzr.at[h, d - 1], zpeer[d])

    def finish(h):
        total = fsum[h, part_of(z * OWN, OWN, OWN), :]
        for d in FAR_FIRST:
            arrival(h * PER_HALF + HZ + d - 1, hzr.at[h, d - 1])
            total = total + hzr[h, d - 1].astype(F32)
        hist_ref[:, h * W:(h + 1) * W] = total

    last_rows(0)
    last_rows(1)

    total = lzs[z]
    for d in FAR_FIRST:
        arrival(LZ + d - 1, lzr.at[d - 1])
        total = total + lzr[d - 1]
    lvz[z] = total[:, :L] / (total[:, L:] + ridge_term)
    for d in FAR_FIRST:
        go(VZ + d - 1, lvz.at[z], lvz.at[z], zpeer[d])

    x_first(0)
    x_first(1)
    x_second(0)
    x_second(1)
    for d in FAR_FIRST:
        arrival(VZ + d - 1, lvz.at[step(z, NZ - d, NZ)])
    lv[c, x] = jnp.concatenate([lvz[i] for i in range(NZ)], axis=0).astype(BF16)
    for d in (2, 1, 3, 0):
        go(VX + 3 + d, lv.at[c, x], lv.at[c, x], other[d])
        if d:
            go(VX + d - 1, lv.at[c, x], lv.at[c, x], xpeer[d])
    z_only(0)
    z_only(1)
    finish(0)
    for d in range(NX):
        arrival(VX + 3 + d, lv.at[1 - c, step(x, NX - d, NX)])
        if d:
            arrival(VX + d - 1, lv.at[c, step(x, NX - d, NX)])

    table = jnp.concatenate([lv[i, j] for i in range(NC) for j in range(NX)], axis=0)
    spot = lax.broadcasted_iota(jnp.int32, (LEAVES, LEAVES), 1)
    label = lax.broadcasted_iota(jnp.int32, (LEAVES, LEAVES), 0)
    swap = jnp.where(leaf_of(spot) == label, 1.0, 0.0).astype(BF16)
    value_ref[...] = jnp.dot(swap, table, preferred_element_type=F32)

    for q in range(NY):
        rows = pl.ds(q * Q, Q)
        looked_up = lax.dot_general(hot[:, rows], table, (((0,), (0,)), ((), ())),
                                    preferred_element_type=F32)
        upd_ref[rows, :] = (pred[rows, :].astype(F32) + shrinkage * looked_up).astype(BF16)
    finish(1)
    for cp in started:
        cp.wait_send()


def store(hist_ref, value_ref, upd_ref, hist_out, value_out, upd_out, sem):
    pairs = ((upd_ref, upd_out), (value_ref, value_out), (hist_ref, hist_out))
    copies = [pltpu.make_async_copy(src, dst, sem.at[i]) for i, (src, dst) in enumerate(pairs)]
    for cp in copies:
        cp.start()
    for cp in copies:
        cp.wait()


def local(predictions, labels, feature_codes, leaf_index, sketch_weight):
    def vmem(*shape, kind=BF16):
        return pltpu.VMEM(shape, kind)

    hist, values, updated = pl.pallas_call(
        kernel,
        out_shape=(vmem(OWN, K, kind=F32), vmem(LEAVES, L, kind=F32), vmem(R, L)),
        in_specs=[pl.BlockSpec(memory_space=pl.ANY)] * 5,
        out_specs=[pl.BlockSpec(memory_space=pltpu.VMEM)] * 3,
        scratch_shapes=[
            vmem(R, L), vmem(R, L), vmem(F, R, kind=jnp.int32), vmem(R, kind=jnp.int32), vmem(L, K),
            vmem(R, L), vmem(R, L), vmem(HALVES, NY, Q, W), vmem(HALVES, 2, H, W), vmem(HALVES, 2, 2, H, W),
            vmem(HALVES, 2, H, W), vmem(HALVES, NY, Q, W), vmem(LEAVES, R), vmem(BINS * F, R),
            vmem(LEAVES, 2 * L, kind=F32), vmem(NX, 8, 2 * L), vmem(NX, 8, 2 * L), vmem(3, 8, 2 * L),
            vmem(3, 8, 2 * L), vmem(NZ, 1, 2 * L, kind=F32), vmem(NZ - 1, 1, 2 * L, kind=F32),
            vmem(NZ, 1, L, kind=F32), vmem(NC, NX, 8, L),
            vmem(HALVES, BINS * F, W, kind=F32), vmem(HALVES, NX, PIECE, W), vmem(HALVES, NX, PIECE, W),
            vmem(HALVES, 4, PIECE // 2, W), vmem(HALVES, 2, PIECE // 2, W), vmem(HALVES, 2, 2, PIECE // 2, W),
            vmem(HALVES, 2, PIECE // 2, W), vmem(HALVES, PIECE, W, kind=F32),
            vmem(HALVES, NZ - 1, OWN, W), vmem(HALVES, NZ - 1, OWN, W),
            pltpu.SemaphoreType.DMA((19,)), pltpu.SemaphoreType.DMA((COPIES,)), pltpu.SemaphoreType.DMA((COPIES,)),
        ],
        compiler_params=pltpu.CompilerParams(
            collective_id=0, has_side_effects=True, vmem_limit_bytes=52 * 2**20),
        name="boost",
    )(predictions, labels, feature_codes, leaf_index, sketch_weight)
    hist, values, updated = pl.pallas_call(
        store,
        out_shape=(
            jax.ShapeDtypeStruct((OWN, K), F32),
            jax.ShapeDtypeStruct((LEAVES, L), F32),
            jax.ShapeDtypeStruct((R, L), BF16),
        ),
        in_specs=[pl.BlockSpec(memory_space=pltpu.VMEM)] * 3,
        out_specs=[pl.BlockSpec(memory_space=pl.ANY)] * 3,
        scratch_shapes=[pltpu.SemaphoreType.DMA((3,))],
        compiler_params=pltpu.CompilerParams(vmem_limit_bytes=2**20),
        name="store",
    )(hist, values, updated)
    return hist.reshape(BINS // LEAVES, F, K), values, updated


def solution(mesh):
    return jax.shard_map(
        local,
        mesh=mesh,
        in_specs=(
            P("rows", "feat"),
            P("rows", "feat"),
            P("feat", "rows"),
            P("rows"),
            P("feat", None),
        ),
        out_specs=(P("rows", "feat", None), P(None, "feat"), P("rows", "feat")),
        check_vma=False,
    )
```

time: 282 us -> 44.6 us (0.16)
  waiting for transfers between devices: 238 us -> 0 us
  Pallas kernels: 0 us -> 43.9 us
  matrix products: 18.4 us -> 0 us
  between operations: 14.1 us -> 0.64 us
  other arithmetic: 6.02 us -> 0 us
  local copies, waits for them, and re-layouts: 3.16 us -> 0 us
    psum x2 -> x0, waiting for transfers between devices: 238 us -> none  [the longest x1 192 us: local(): lax.psum(jnp.einsum('bfr,rk->bfk', one_hot, sketch, preferred_element_typ...]
    pallas_call x0 -> x2, Pallas kernels: none -> 43.9 us  [the longest x1 42.1 us: local(): pl.pallas_call(kernel, out_shape=(vmem(OWN, K, kind=F32), vmem(LEAVES, L,...]
    dot_general x5 -> x0, matrix products: 18.4 us -> none  [the longest x1 5.75 us: local(): jnp.einsum('lr,lc->rc', leaf_hot.astype(jnp.float32), leaf_values, precis...]
    convert_element_type x1 -> x0, other arithmetic: 4.95 us -> none  [local(): gradient = (labels.astype(jnp.float32) - probability).astype(jnp.bfloat16)]
  transfers between devices with their start and end apart: 2 -> 0, of which waited for: 2 -> 0; matrix products, arithmetic and copies ran while one was open for 2% -> 0% of each run, Pallas kernels for 0% -> 0%
where the time goes in v2:
time: 44.6 us; the launch traced here: 44.5 us
  Pallas kernels  43.9 us (98%)
  between operations  0.64 us (1%)
    pallas_call x1, Pallas kernels, local(): pl.pallas_call(kernel, out_shape=(vmem(OWN, K, kind=F32), vmem(LEAVES, L,...  42.1 us
    pallas_call x1, Pallas kernels, local(): pl.pallas_call(store, out_shape=(jax.ShapeDtypeStruct((OWN, K), F32), jax...  1.77 us

profile of v2, /device:TPU:6, one launch (start us, length us, event | category | flops | bytes accessed | tf_op | source)
XLA Modules:
  0.0 44.5 jit_solution(9636298258665263058)
XLA Ops:
  0.6 42.1 %boost.1 = (f32[32,256]{1,0:T(8,128)S(1)}, f32[64,1024]{1,0:T(8,128)S(1)}, bf16[1536,1024]{1,0:T(8,128)(2,1)S(1)}) custom-call(bf16[1536,1024]{1,0:T(8,128)(2,1)} %pred_hbm.1, bf16[1536,1024]{1,0:T(8,128)(2,1)} %lab_hbm.1, s32[8,1536]{1,0:T(8,128)} %codes_hbm.1, s32[1536]{0:T(1024)} %leaf_hbm.1, bf16[1024,256]{1,0:T(8,128)(2,1)} %w_hbm.1), custom_call_target="tpu_custom_call" | custom-call | tf_op jit(solution)/shard_map/boost/pallas_call | solution.py:366
  42.8 1.8 %store.1 = (f32[32,256]{1,0:T(8,128)}, f32[64,1024]{1,0:T(8,128)}, bf16[1536,1024]{1,0:T(8,128)(2,1)}) custom-call(f32[32,256]{1,0:T(8,128)S(1)} %get-tuple-element.9.hist_ref, f32[64,1024]{1,0:T(8,128)S(1)} %get-tuple-element.10.value_ref, bf16[1536,1024]{1,0:T(8,128)(2,1)S(1)} %get-tuple-element.11.upd_ref), custom_call_target="tpu_custom_call" | custom-call | tf_op jit(solution)/shard_map/store/pallas_call | solution.py:388

commit v3 on v2

--- a/solution.py
+++ b/solution.py
@@ -22,8 +22,8 @@
 shrinkage = 0.5
 ridge_term = 1.0
 
-RS, AG, HC, HX, HZ, PER_HALF = 0, 6, 12, 16, 22, 29
-LC, LX, LZ, VZ, VX, COPIES = 58, 59, 62, 69, 76, 83
+RS, AG, HC, HX, HZ, PER_HALF = 0, 6, 12, 16, 19, 26
+LC, LX, LZ, VZ, VX, COPIES = 52, 53, 56, 63, 70, 77
 FAR_FIRST = (4, 3, 5, 2, 6, 1, 7)
 XORDER = (2, 1, 3, 0)
 
@@ -36,7 +36,7 @@
            hist_ref, value_ref, upd_ref,
            pred, lab, codes, leaf, w, grad, hess, part, rs1, rs2, rsum, sk, hot, oh,
            lsum, lcs, lcr, lxs, lxr, lzs, lzr, lvz, lv,
-           acc, hcs, hcr, hxs, hx1, hx2, hxsum, fsum, hzs, hzr,
+           acc, hcs, hcr, hxs, hxr, fsum, hzs, hzr,
            load_sem, send, recv):
     row = lax.axis_index("rows")
     y = lax.axis_index("feat")
@@ -55,7 +55,7 @@
     xpeer = [(at(z, step(x, d, NX), c), y) for d in range(NX)]
     zpeer = [(at(step(z, d, NZ), x, c), y) for d in range(NZ)]
     other = [(at(z, step(x, d, NX), 1 - c), y) for d in range(NX)]
-    started = []
+    started = {}
 
     def copy(n, src, dst, to):
         return pltpu.make_async_remote_copy(
@@ -63,9 +63,8 @@
             device_id=to, device_id_type=MESH)
 
     def go(n, src, dst, to):
-        cp = copy(n, src, dst, to)
-        cp.start()
-        started.append(cp)
+        copy(n, src, dst, to).start()
+        started.setdefault(n, (src, dst, to))
 
     def arrival(n, dst):
         copy(n, dst, dst, partner).wait_recv()
@@ -75,8 +74,6 @@
 
     barrier = pltpu.get_barrier_semaphore()
     peers = other + ypeer[1::2] + xpeer[1:] + zpeer[1:]
-    for peer in peers:
-        pl.semaphore_signal(barrier, inc=1, device_id=peer, device_id_type=MESH)
 
     order = [step(y, 2, NY), step(y, 1, NY), step(y, 3, NY), y]
     w_load = pltpu.make_async_copy(w_hbm, w, load_sem.at[16])
@@ -93,6 +90,8 @@
             cp.start()
         if n == 1:
             w_load.start()
+            for peer in peers:
+                pl.semaphore_signal(barrier, inc=1, device_id=peer, device_id_type=MESH)
     leaf_load.start()
     codes_load.start()
 
@@ -233,8 +232,10 @@
             acc[h, rows, :] = acc[h, rows, :] + terms(h, 1, 3, rows)
 
     start_terms(0)
+    forward(0)
     start_terms(1)
-    forward(0)
+    side_terms(0)
+    forward(1)
     for d in (1, 2, 3):
         arrival(LX + d - 1, lxr.at[d - 1])
     mine = lsum[part_of(x * 8, 8, 8), :]
@@ -244,9 +245,6 @@
         lzs[i] = mine[i:i + 1, :]
     for d in FAR_FIRST:
         go(LZ + d - 1, lzs.at[step(z, d, NZ)], lzr.at[d - 1], zpeer[d])
-    side_terms(0)
-    forward(1)
-    side_terms(1)
 
     def last_rows(h):
         arrival(h * PER_HALF + AG + 4, sk_at(h, 3, top))
@@ -259,40 +257,22 @@
         for rows in tiles[NX:]:
             acc[h, rows, :] = acc[h, rows, :] + terms(h, 3, 4, rows)
 
-    half = PIECE // 2
-    up, down = pl.ds(0, half), pl.ds(half, half)
-
-    def both_cores(h, i, n):
-        return acc[h, pl.ds(CORE + i * PIECE + n * half, half), :] + hcr[h, i, pl.ds(n * half, half), :].astype(F32)
-
-    def x_first(h):
-        for i in range(NX):
+    def both_cores(h, i):
+        return acc[h, tiles[NX + i], :] + hcr[h, i].astype(F32)
+
+    def x_only(h):
+        for i, d in enumerate(XORDER):
             arrival(h * PER_HALF + HC + i, hcr.at[h, i])
-            if i == 0:
-                hxs[h, 0] = both_cores(h, 0, 0).astype(BF16)
-                hxs[h, 1] = both_cores(h, 0, 1).astype(BF16)
-                go(h * PER_HALF + HX + 0, hxs.at[h, 0], hx1.at[h, 0], xpeer[1])
-                go(h * PER_HALF + HX + 1, hxs.at[h, 1], hx1.at[h, 1], xpeer[3])
-            if i == 1:
-                hxs[h, 2] = both_cores(h, 1, 1).astype(BF16)
-                go(h * PER_HALF + HX + 2, hxs.at[h, 2], hx2.at[h, 0, 1], xpeer[1])
-            if i == 2:
-                hxs[h, 3] = both_cores(h, 2, 0).astype(BF16)
-                go(h * PER_HALF + HX + 3, hxs.at[h, 3], hx2.at[h, 1, 0], xpeer[3])
-
-    def x_second(h):
-        for n, i, to in ((0, 1, 1), (1, 2, 3)):
-            arrival(h * PER_HALF + HX + n, hx1.at[h, n])
-            hxsum[h, n] = (both_cores(h, i, n) + hx1[h, n].astype(F32)).astype(BF16)
-            go(h * PER_HALF + HX + 4 + n, hxsum.at[h, n], hx2.at[h, n, n], xpeer[to])
+            if d:
+                hxs[h, i] = both_cores(h, i).astype(BF16)
+                go(h * PER_HALF + HX + i, hxs.at[h, i], hxr.at[h, i], xpeer[d])
 
     def z_only(h):
-        for n in range(2):
-            arrival(h * PER_HALF + HX + 4 + n, hx2.at[h, n, n])
-            arrival(h * PER_HALF + HX + 3 - n, hx2.at[h, 1 - n, n])
-        for n in range(2):
-            fsum[h, pl.ds(n * half, half), :] = (
-                both_cores(h, 3, n) + hx2[h, 0, n].astype(F32) + hx2[h, 1, n].astype(F32))
+        total = both_cores(h, NX - 1)
+        for i in range(NX - 1):
+            arrival(h * PER_HALF + HX + i, hxr.at[h, i])
+            total = total + hxr[h, i].astype(F32)
+        fsum[h] = total
         for d in FAR_FIRST:
             hzs[h, d - 1] = fsum[h, part_of(step(z, d, NZ) * OWN, OWN, OWN), :].astype(BF16)
             go(h * PER_HALF + HZ + d - 1, hzs.at[h, d - 1], hzr.at[h, d - 1], zpeer[d])
@@ -304,8 +284,13 @@
             total = total + hzr[h, d - 1].astype(F32)
         hist_ref[:, h * W:(h + 1) * W] = total
 
+    for i, d in enumerate(XORDER[:NX - 1]):
+        started[HX + i] = (hxs.at[0, i], hxr.at[0, i], xpeer[d])
     last_rows(0)
+    side_terms(1)
+    pl.when(c == 0)(lambda: x_only(0))
     last_rows(1)
+    pl.when(c == 1)(lambda: x_only(0))
 
     total = lzs[z]
     for d in FAR_FIRST:
@@ -315,10 +300,8 @@
     for d in FAR_FIRST:
         go(VZ + d - 1, lvz.at[z], lvz.at[z], zpeer[d])
 
-    x_first(0)
-    x_first(1)
-    x_second(0)
-    x_second(1)
+    x_only(1)
+
     for d in FAR_FIRST:
         arrival(VZ + d - 1, lvz.at[step(z, NZ - d, NZ)])
     lv[c, x] = jnp.concatenate([lvz[i] for i in range(NZ)], axis=0).astype(BF16)
@@ -328,7 +311,6 @@
             go(VX + d - 1, lv.at[c, x], lv.at[c, x], xpeer[d])
     z_only(0)
     z_only(1)
-    finish(0)
     for d in range(NX):
         arrival(VX + 3 + d, lv.at[1 - c, step(x, NX - d, NX)])
         if d:
@@ -345,13 +327,16 @@
         looked_up = lax.dot_general(hot[:, rows], table, (((0,), (0,)), ((), ())),
                                     preferred_element_type=F32)
         upd_ref[rows, :] = (pred[rows, :].astype(F32) + shrinkage * looked_up).astype(BF16)
+    finish(0)
     finish(1)
-    for cp in started:
-        cp.wait_send()
+    for n, (src, dst, to) in started.items():
+        copy(n, src, dst, to).wait_send()
 
 
 def store(hist_ref, value_ref, upd_ref, hist_out, value_out, upd_out, sem):
-    pairs = ((upd_ref, upd_out), (value_ref, value_out), (hist_ref, hist_out))
+    blocks = [pl.ds(i * Q, Q) for i in range(NY)]
+    pairs = [(upd_ref.at[rows], upd_out.at[rows]) for rows in blocks]
+    pairs += [(value_ref, value_out), (hist_ref, hist_out)]
     copies = [pltpu.make_async_copy(src, dst, sem.at[i]) for i, (src, dst) in enumerate(pairs)]
     for cp in copies:
         cp.start()
@@ -376,8 +361,7 @@
             vmem(3, 8, 2 * L), vmem(NZ, 1, 2 * L, kind=F32), vmem(NZ - 1, 1, 2 * L, kind=F32),
             vmem(NZ, 1, L, kind=F32), vmem(NC, NX, 8, L),
             vmem(HALVES, BINS * F, W, kind=F32), vmem(HALVES, NX, PIECE, W), vmem(HALVES, NX, PIECE, W),
-            vmem(HALVES, 4, PIECE // 2, W), vmem(HALVES, 2, PIECE // 2, W), vmem(HALVES, 2, 2, PIECE // 2, W),
-            vmem(HALVES, 2, PIECE // 2, W), vmem(HALVES, PIECE, W, kind=F32),
+            vmem(HALVES, NX - 1, PIECE, W), vmem(HALVES, NX - 1, PIECE, W), vmem(HALVES, PIECE, W, kind=F32),
             vmem(HALVES, NZ - 1, OWN, W), vmem(HALVES, NZ - 1, OWN, W),
             pltpu.SemaphoreType.DMA((19,)), pltpu.SemaphoreType.DMA((COPIES,)), pltpu.SemaphoreType.DMA((COPIES,)),
         ],
@@ -394,7 +378,7 @@
         ),
         in_specs=[pl.BlockSpec(memory_space=pltpu.VMEM)] * 3,
         out_specs=[pl.BlockSpec(memory_space=pl.ANY)] * 3,
-        scratch_shapes=[pltpu.SemaphoreType.DMA((3,))],
+        scratch_shapes=[pltpu.SemaphoreType.DMA((NY + 2,))],
         compiler_params=pltpu.CompilerParams(vmem_limit_bytes=2**20),
         name="store",
     )(hist, values, updated)

time: 44.6 us -> 42.6 us (0.955)
  the two profiles are of different devices: /device:TPU:6 before, /device:TPU:1 now
where the time goes in v3:
time: 42.6 us; the launch traced here: 42.5 us
  Pallas kernels  41.8 us (98%)
  between operations  0.64 us (2%)
    pallas_call x1, Pallas kernels, local(): pl.pallas_call(kernel, out_shape=(vmem(OWN, K, kind=F32), vmem(LEAVES, L,...  40.1 us
    pallas_call x1, Pallas kernels, local(): pl.pallas_call(store, out_shape=(jax.ShapeDtypeStruct((OWN, K), F32), jax...  1.79 us

profile of v3, /device:TPU:1, one launch (start us, length us, event | category | flops | bytes accessed | tf_op | source)
XLA Modules:
  0.0 42.5 jit_solution(17822437328353355766)
XLA Ops:
  0.6 40.1 %boost.1 = (f32[32,256]{1,0:T(8,128)S(1)}, f32[64,1024]{1,0:T(8,128)S(1)}, bf16[1536,1024]{1,0:T(8,128)(2,1)S(1)}) custom-call(bf16[1536,1024]{1,0:T(8,128)(2,1)} %pred_hbm.1, bf16[1536,1024]{1,0:T(8,128)(2,1)} %lab_hbm.1, s32[8,1536]{1,0:T(8,128)} %codes_hbm.1, s32[1536]{0:T(1024)} %leaf_hbm.1, bf16[1024,256]{1,0:T(8,128)(2,1)} %w_hbm.1), custom_call_target="tpu_custom_call" | custom-call | tf_op jit(solution)/shard_map/boost/pallas_call | solution.py:351
  40.7 1.8 %store.1 = (f32[32,256]{1,0:T(8,128)}, f32[64,1024]{1,0:T(8,128)}, bf16[1536,1024]{1,0:T(8,128)(2,1)}) custom-call(f32[32,256]{1,0:T(8,128)S(1)} %get-tuple-element.9.hist_ref, f32[64,1024]{1,0:T(8,128)S(1)} %get-tuple-element.10.value_ref, bf16[1536,1024]{1,0:T(8,128)(2,1)S(1)} %get-tuple-element.11.upd_ref), custom_call_target="tpu_custom_call" | custom-call | tf_op jit(solution)/shard_map/store/pallas_call | solution.py:372

commit v4 on v3

--- a/solution.py
+++ b/solution.py
@@ -204,16 +204,22 @@
 
     lax.fori_loop(0, NZ, bins_of, 0)
 
-    arrival(LC, lcr)
-    kept = lsum[part_of(c * 32, 32, 32), :]
-    for i in range(NX):
-        lsum[pl.ds(i * 8, 8), :] = kept[i * 8:(i + 1) * 8, :] + lcr[i].astype(F32)
-    for d in (2, 1, 3):
-        lxs[d - 1] = lsum[part_of(step(x, d, NX) * 8, 8, 8), :].astype(BF16)
-        go(LX + d - 1, lxs.at[d - 1], lxr.at[d - 1], xpeer[d])
-
+    for d in (1, 2, 3):
+        started[LX + d - 1] = (lxs.at[d - 1], lxr.at[d - 1], xpeer[d])
+
+    def leaf_x():
+        arrival(LC, lcr)
+        kept = lsum[part_of(c * 32, 32, 32), :]
+        for i in range(NX):
+            lsum[pl.ds(i * 8, 8), :] = kept[i * 8:(i + 1) * 8, :] + lcr[i].astype(F32)
+        for d in (2, 1, 3):
+            lxs[d - 1] = lsum[part_of(step(x, d, NX) * 8, 8, 8), :].astype(BF16)
+            go(LX + d - 1, lxs.at[d - 1], lxr.at[d - 1], xpeer[d])
+
+    pl.when(c == 0)(leaf_x)
     own_sketch(1)
     own_rest(1)
+    pl.when(c == 1)(leaf_x)
 
     def terms(h, first, last, rows):
         sketch = sk[h, first:last].reshape((last - first) * Q, W)

time: 42.6 us -> 42.5 us (level)
  no operation moved by 1% of the time
where the time goes in v4:
time: 42.5 us; the launch traced here: 42.4 us
  Pallas kernels  41.8 us (98%)
  between operations  0.64 us (2%)
    pallas_call x1, Pallas kernels, local(): pl.pallas_call(kernel, out_shape=(vmem(OWN, K, kind=F32), vmem(LEAVES, L,...  40 us
    pallas_call x1, Pallas kernels, local(): pl.pallas_call(store, out_shape=(jax.ShapeDtypeStruct((OWN, K), F32), jax...  1.79 us

profile of v4, /device:TPU:1, one launch (start us, length us, event | category | flops | bytes accessed | tf_op | source)
XLA Modules:
  0.0 42.4 jit_solution(7090119874620857787)
XLA Ops:
  0.6 40.0 %boost.1 = (f32[32,256]{1,0:T(8,128)S(1)}, f32[64,1024]{1,0:T(8,128)S(1)}, bf16[1536,1024]{1,0:T(8,128)(2,1)S(1)}) custom-call(bf16[1536,1024]{1,0:T(8,128)(2,1)} %pred_hbm.1, bf16[1536,1024]{1,0:T(8,128)(2,1)} %lab_hbm.1, s32[8,1536]{1,0:T(8,128)} %codes_hbm.1, s32[1536]{0:T(1024)} %leaf_hbm.1, bf16[1024,256]{1,0:T(8,128)(2,1)} %w_hbm.1), custom_call_target="tpu_custom_call" | custom-call | tf_op jit(solution)/shard_map/boost/pallas_call | solution.py:357
  40.6 1.8 %store.1 = (f32[32,256]{1,0:T(8,128)}, f32[64,1024]{1,0:T(8,128)}, bf16[1536,1024]{1,0:T(8,128)(2,1)}) custom-call(f32[32,256]{1,0:T(8,128)S(1)} %get-tuple-element.9.hist_ref, f32[64,1024]{1,0:T(8,128)S(1)} %get-tuple-element.10.value_ref, bf16[1536,1024]{1,0:T(8,128)(2,1)S(1)} %get-tuple-element.11.upd_ref), custom_call_target="tpu_custom_call" | custom-call | tf_op jit(solution)/shard_map/store/pallas_call | solution.py:378
